TPU v7x, 32 devices: a whole 2x2x4 slice. The times are simulated.
32 devices in a mesh: seq: 8 (over y, x, core), head: 4 (over z).
Axes of the slice: x: 2, y: 2, z: 4, core: 2. Of those that a mesh axis runs over, the one named last changes fastest.
Arguments:
- teacher_query: bfloat16 [7168, 1024], P(('seq', 'head')), may hold values from -96 to 96
- teacher_key: bfloat16 [7168, 1024], P(('seq', 'head')), may hold values from -96 to 96
- teacher_value: bfloat16 [7168, 1024], P(('seq', 'head')), may hold values from -96 to 96
- student_query: bfloat16 [7168, 768], P(('seq', 'head')), may hold values from -96 to 96
- student_key: bfloat16 [7168, 768], P(('seq', 'head')), may hold values from -96 to 96
- student_value: bfloat16 [7168, 768], P(('seq', 'head')), may hold values from -96 to 96
Outputs:
- grad_query: bfloat16 [7168, 768], P(('seq', 'head'))
- grad_key: bfloat16 [7168, 768], P(('seq', 'head'))
- grad_value: bfloat16 [7168, 768], P(('seq', 'head'))
- loss: float32 [], replicated
All inputs are finite; a program needn't handle non-finite values.
Results may differ from a plain program's by a relative error of at most 0.0051.
Values may be sent and summed in bfloat16 or wider, within the bound.
A program may use at most 128 MiB of HBM per device.

v0:
```python
import jax
import jax.numpy as jnp
from jax import lax
from jax.sharding import PartitionSpec as P

HEADS = 16
TD = 64
SD = 48


def logits(left, right, scale):
    return jnp.einsum("rhd,chd->hrc", left, right, preferred_element_type=jnp.float32) * scale


def over_blocks(step, carry, piece):
    count = piece[0].shape[0]
    size = 1024
    turns = count // size

    def advance(index, state):
        sub = tuple((lax.dynamic_slice_in_dim(member, index * size, size, 0) for member in piece))
        return step(state, sub, index * size)

    return lax.fori_loop(0, turns, advance, carry)


def on_device(teacher_query, teacher_key, teacher_value, student_query, student_key, student_value):
    teach_q, teach_k, teach_v, stud_q, stud_k, stud_v = (
        lax.all_to_all(teacher_query, "head", split_axis=1, concat_axis=0, tiled=True),
        lax.all_to_all(teacher_key, "head", split_axis=1, concat_axis=0, tiled=True),
        lax.all_to_all(teacher_value, "head", split_axis=1, concat_axis=0, tiled=True),
        lax.all_to_all(student_query, "head", split_axis=1, concat_axis=0, tiled=True),
        lax.all_to_all(student_key, "head", split_axis=1, concat_axis=0, tiled=True),
        lax.all_to_all(student_value, "head", split_axis=1, concat_axis=0, tiled=True),
    )
    rows = teach_q.shape[0]
    local_heads = teach_q.shape[1] // TD
    total_rows = rows * lax.axis_size("seq")
    tscale = TD ** (-0.5)
    sscale = SD ** (-0.5)
    query_t = teach_q.reshape(rows, local_heads, TD)
    value_t = teach_v.reshape(rows, local_heads, TD)
    query_s = stud_q.reshape(rows, local_heads, SD)
    value_s = stud_v.reshape(rows, local_heads, SD)
    key_set = (teach_k, teach_v, stud_k, stud_v)

    def unpack(piece):
        count = piece[0].shape[0]
        return (
            piece[0].reshape(count, local_heads, TD),
            piece[1].reshape(count, local_heads, TD),
            piece[2].reshape(count, local_heads, SD),
            piece[3].reshape(count, local_heads, SD),
        )

    def stats_step(carry, piece, start):
        far_tk, far_tv, far_sk, far_sv = unpack(piece)
        blocks = (
            logits(query_t, far_tk, tscale),
            logits(value_t, far_tv, tscale),
            logits(query_s, far_sk, sscale),
            logits(value_s, far_sv, sscale),
        )
        updated = []
        for (peak, mass), score in zip(carry, blocks):
            top = jnp.maximum(peak, jnp.max(score, axis=-1))
            mass = mass * jnp.exp(peak - top) + jnp.sum(jnp.exp(score - top[..., None]), axis=-1)
            updated.append((top, mass))
        return tuple(updated)

    blank = (
        jnp.full((local_heads, rows), -1e30, jnp.float32),
        jnp.zeros((local_heads, rows), jnp.float32),
    )
    stats_init = (blank, blank, blank, blank)
    stats = over_blocks(
        stats_step,
        stats_init,
        (
            lax.all_gather(key_set[0], "seq", axis=0, tiled=True),
            lax.all_gather(key_set[1], "seq", axis=0, tiled=True),
            lax.all_gather(key_set[2], "seq", axis=0, tiled=True),
            lax.all_gather(key_set[3], "seq", axis=0, tiled=True),
        ),
    )
    norm_a, norm_b, norm_c, norm_e = [(peak + jnp.log(mass))[..., None] for peak, mass in stats]

    def grads_step(carry, piece, start):
        acc_q, acc_v, total = (carry[0], carry[1], carry[-1])
        far_tk, far_tv, far_sk, far_sv = unpack(piece)
        count = far_tk.shape[0]
        log_a = logits(query_t, far_tk, tscale) - norm_a
        log_b = logits(value_t, far_tv, tscale) - norm_b
        log_c = logits(query_s, far_sk, sscale) - norm_c
        log_e = logits(value_s, far_sv, sscale) - norm_e
        prob_a = jnp.exp(log_a)
        prob_b = jnp.exp(log_b)
        total = (
            total
            + jnp.sum(prob_a * (log_a - log_c), axis=-1)
            + jnp.sum(prob_b * (log_b - log_e), axis=-1)
        )
        grad_qk = (jnp.exp(log_c) - prob_a).astype(jnp.bfloat16)
        grad_vv = (jnp.exp(log_e) - prob_b).astype(jnp.bfloat16)
        acc_q = (
            acc_q
            + jnp.einsum("hrc,chd->rhd", grad_qk, far_sk, preferred_element_type=jnp.float32)
            * sscale
        )
        acc_v = (
            acc_v
            + jnp.einsum("hrc,chd->rhd", grad_vv, far_sv, preferred_element_type=jnp.float32)
            * sscale
        )
        full_k, full_v = (carry[2], carry[3])
        part_k = (
            jnp.einsum("hrc,rhd->chd", grad_qk, query_s, preferred_element_type=jnp.float32)
            * sscale
        )
        part_v = (
            jnp.einsum("hrc,rhd->chd", grad_vv, value_s, preferred_element_type=jnp.float32)
            * sscale
        )
        full_k = lax.dynamic_update_slice_in_dim(
            full_k, lax.dynamic_slice_in_dim(full_k, start, count, 0) + part_k, start, 0
        )
        full_v = lax.dynamic_update_slice_in_dim(
            full_v, lax.dynamic_slice_in_dim(full_v, start, count, 0) + part_v, start, 0
        )
        return (acc_q, acc_v, full_k, full_v, total)

    row_zeros = jnp.zeros((rows, local_heads, SD), jnp.float32)
    loss_zeros = jnp.zeros((local_heads, rows), jnp.float32)
    grads_init = (
        row_zeros,
        row_zeros,
        jnp.zeros((total_rows, local_heads, SD), jnp.float32),
        jnp.zeros((total_rows, local_heads, SD), jnp.float32),
        loss_zeros,
    )
    results = over_blocks(
        grads_step,
        grads_init,
        (
            lax.all_gather(key_set[0], "seq", axis=0, tiled=True),
            lax.all_gather(key_set[1], "seq", axis=0, tiled=True),
            lax.all_gather(key_set[2], "seq", axis=0, tiled=True),
            lax.all_gather(key_set[3], "seq", axis=0, tiled=True),
        ),
    )
    acc_q, acc_v, total = (results[0], results[1], results[-1])
    owned_k, owned_v = (
        lax.psum_scatter(results[2], "seq", scatter_dimension=0, tiled=True),
        lax.psum_scatter(results[3], "seq", scatter_dimension=0, tiled=True),
    )
    out_q = acc_q.astype(jnp.bfloat16).reshape(rows, local_heads * SD)
    out_k = owned_k.astype(jnp.bfloat16).reshape(rows, local_heads * SD)
    out_v = (acc_v + owned_v).astype(jnp.bfloat16).reshape(rows, local_heads * SD)
    grad_query, grad_key, grad_value = (
        lax.all_to_all(out_q, "head", split_axis=0, concat_axis=1, tiled=True),
        lax.all_to_all(out_k, "head", split_axis=0, concat_axis=1, tiled=True),
        lax.all_to_all(out_v, "head", split_axis=0, concat_axis=1, tiled=True),
    )
    loss = lax.psum(jnp.sum(total), ("seq", "head")) / (HEADS * total_rows)
    return (grad_query, grad_key, grad_value, loss)


def solution(mesh):
    in_specs = (
        P(("seq", "head"), None),
        P(("seq", "head"), None),
        P(("seq", "head"), None),
        P(("seq", "head"), None),
        P(("seq", "head"), None),
        P(("seq", "head"), None),
    )
    out_specs = (P(("seq", "head"), None), P(("seq", "head"), None), P(("seq", "head"), None), P())
    return jax.shard_map(
        on_device, mesh=mesh, in_specs=in_specs, out_specs=out_specs, check_vma=False
    )
```

profile of v0, /device:TPU:0, one launch (start us, length us, event | category | flops | bytes accessed | tf_op | source)
XLA Modules:
  0.0 1050.0 jit_solution(8232869181207322607)
XLA Ops:
  8.3 19.3 %all_to_all.165 = bf16[224,4,256]{2,0,1:T(8,128)(2,1)} all-to-all(bf16[224,4,256]{2,0,1:T(8,128)(2,1)S(1)} %bitcast.253), channel_id=1, replica_groups=mesh['seq'=8,'head'=4] {'head'}, dimensions={1} | all-to-all | bytes 917504 | tf_op jit(solution)/shard_map/all_to_all | solution.py:30
  28.7 15.6 %all_to_all.166 = bf16[224,4,256]{2,0,1:T(8,128)(2,1)} all-to-all(bf16[224,4,256]{2,0,1:T(8,128)(2,1)S(1)} %bitcast.254), channel_id=1, replica_groups=mesh['seq'=8,'head'=4] {'head'}, dimensions={1} | all-to-all | bytes 917504 | tf_op jit(solution)/shard_map/all_to_all | solution.py:31
  45.6 13.4 %all_to_all.167 = bf16[224,4,192]{0,2,1:T(8,128)(2,1)S(1)} all-to-all(bf16[224,4,192]{0,2,1:T(8,128)(2,1)S(1)} %bitcast.262), channel_id=1, replica_groups=mesh['seq'=8,'head'=4] {'head'}, dimensions={1} | all-to-all | bytes 688128 | tf_op jit(solution)/shard_map/all_to_all | solution.py:33
  61.6 13.7 %all_to_all.168 = bf16[224,4,192]{0,2,1:T(8,128)(2,1)S(1)} all-to-all(bf16[224,4,192]{0,2,1:T(8,128)(2,1)S(1)} %bitcast.263), channel_id=1, replica_groups=mesh['seq'=8,'head'=4] {'head'}, dimensions={1} | all-to-all | bytes 688128 | tf_op jit(solution)/shard_map/all_to_all | solution.py:34
  83.8 8.7 all-to-all-done.1
  97.0 10.2 all-to-all-done.3
  120.4 10.5 all-gather.5.cloned.1.call-done
  130.9 33.0 %all-gather.11.cloned.1.call-done = bf16[7168,192]{0,1:T(8,128)(2,1)} async-done(((bf16[896,192]{0,1:T(8,128)(2,1)}), bf16[7168,192]{0,1:T(8,128)(2,1)}) %all-gather.11.cloned.1.call-update) | async-done | bytes 2752528 | tf_op jit(solution)/shard_map/all_gather | solution.py:148
  163.9 458.7 %while.50 = (s32[]{:T(128)}, f32[4,896]{1,0:T(4,128)S(1)}, f32[4,896]{1,0:T(4,128)S(1)}, f32[4,896]{1,0:T(4,128)S(1)}, f32[4,896]{1,0:T(4,128)S(1)}, /*index=5*/...) while((s32[]{:T(128)}, f32[4,896]{1,0:T(4,128)S(1)}, ...), condition=%wide.region_9.0_spmd.clone, body=%wide.region_0.0_spmd.clone.sunk | while | flops 1717639168 | bytes 125296912 | solution.py:24
  205.5 7.6 fusion.98
  220.4 7.6 fusion.97
  269.5 7.6 fusion.98
  284.4 7.6 fusion.97
  628.8 242.6 %while.51 = (s32[]{:T(128)}, f32[896,4,48]{0,2,1:T(8,128)}, f32[896,4,48]{0,2,1:T(8,128)S(1)}, f32[7168,4,48]{0,2,1:T(8,128)}, f32[7168,4,48]{0,2,1:T(8,128)}, /...) while((s32[]{:T(128)}, f32[896,4,48]{0,2,1:T(8,128)}, ...), condition=%wide.region_13.0_spmd.clone, body=%wide.region_10.0_spmd.clone.sunk | while | flops 3121335808 | bytes 120140104 | solution.py:24
  648.1 7.9 multiply_reduce_fusion.4
  681.8 7.9 multiply_reduce_fusion.4
  716.6 7.9 multiply_reduce_fusion.4
  751.5 7.9 multiply_reduce_fusion.4
  786.3 7.9 multiply_reduce_fusion.4
  821.1 7.9 multiply_reduce_fusion.4
  855.9 7.9 multiply_reduce_fusion.4
  878.9 50.5 %reduce-scatter.5.cloned.1.call-done = f32[896,4,48]{0,2,1:T(8,128)} async-done(((f32[7168,4,48]{0,2,1:T(8,128)}), f32[896,4,48]{0,2,1:T(8,128)}) %reduce-scatter.5.cloned.1.call-update) | async-done | bytes 688144 | tf_op jit(solution)/shard_map/reduce_scatter | solution.py:154
  936.3 54.6 %reduce-scatter.3.cloned.1.call-done = f32[896,4,48]{0,2,1:T(8,128)} async-done(((f32[7168,4,48]{0,2,1:T(8,128)}), f32[896,4,48]{0,2,1:T(8,128)}) %reduce-scatter.3.cloned.1.call-update) | async-done | bytes 688144 | tf_op jit(solution)/shard_map/reduce_scatter | solution.py:153
  998.5 40.0 %psum.7 = f32[]{:T(128)} all-reduce(f32[]{:T(128)} %reduce_sum.87), channel_id=1, replica_groups=mesh['seq'=8,'head'=4] {'seq','head'}, use_global_device_ids=true, to_apply=%region_17.0 | all-reduce | flops 1 | bytes 8 | tf_op jit(solution)/shard_map/psum | solution.py:164
  (323 shorter events, 666.5 us)
Async XLA Ops:
  7.2 101.5 %all-gather.7.cloned.1.call-start = ((), (), s32[]{:S(2)}) async-start(), calls=%async_computation.12 | async-start | bytes 4128768 | tf_op jit(solution)/shard_map/all_gather | solution.py:145
  27.6 86.9 %all-gather.9.cloned.1.call-start = ((), (), s32[]{:S(2)}) async-start(), calls=%async_computation.13 | async-start | bytes 4128768 | tf_op jit(solution)/shard_map/all_gather | solution.py:146
  44.3 63.6 %copy-start.3 = (bf16[224,4,256]{2,0,1:T(8,128)(2,1)S(1)}, bf16[224,4,256]{2,0,1:T(8,128)(2,1)}, u32[]{:S(2)}) copy-start(bf16[224,4,256]{2,0,1:T(8,128)(2,1)} %all_to_all.166) | copy-start | bytes 1376260
  44.3 86.6 %all-gather.5.cloned.1.call-start = ((), (), s32[]{:S(2)}) async-start(), calls=%async_computation.11 | async-start | bytes 3096576 | tf_op jit(solution)/shard_map/all_gather | solution.py:147
  60.4 103.5 %all-gather.11.cloned.1.call-start = ((), (), s32[]{:S(2)}) async-start(), calls=%async_computation.14 | async-start | bytes 3096576 | tf_op jit(solution)/shard_map/all_gather | solution.py:148
  78.5 14.0 %all-to-all-start.1 = ((bf16[224,4,192]{0,2,1:T(8,128)(2,1)}), bf16[224,4,192]{0,2,1:T(8,128)(2,1)S(1)}, u32[]{:S(2)}, u32[]{:S(2)}) async-start(bf16[224,4,192]{0,2,1:T(8,128)(2,1)} %bitcast.2), calls=%async_computation.1 | async-start | bytes 786432 | tf_op jit(solution)/shard_map/all_to_all | solution.py:32
  92.5 14.7 %all-to-all-start.3 = ((bf16[224,4,256]{2,0,1:T(8,128)(2,1)}), bf16[224,4,256]{2,0,1:T(8,128)(2,1)S(1)}, u32[]{:S(2)}, u32[]{:S(2)}) async-start(bf16[224,4,256]{2,0,1:T(8,128)(2,1)} %bitcast.142), calls=%async_computation.3 | async-start | bytes 917504 | tf_op jit(solution)/shard_map/all_to_all | solution.py:29
  96.0 833.4 %reduce-scatter.5.cloned.1.call-start = ((), (), s32[]{:S(2)}) async-start(), calls=%async_computation.16 | async-start | bytes 6193152 | tf_op jit(solution)/shard_map/reduce_scatter | solution.py:154
  163.9 464.9 %copy-start.2 = (f32[896,4,48]{0,2,1:T(8,128)S(1)}, f32[896,4,48]{0,2,1:T(8,128)}, u32[]{:S(2)}) copy-start(f32[896,4,48]{0,2,1:T(8,128)} %custom-call.9) | copy-start | bytes 2064388
  163.9 464.9 %copy-start.4 = (f32[4,896]{1,0:T(4,128)S(1)}, f32[4,896]{1,0:T(4,128)}, u32[]{:S(2)}) copy-start(f32[4,896]{1,0:T(4,128)} %custom-call.10) | copy-start | bytes 43012
  628.8 1.3 copy-start
  648.1 10.1 copy-start.1
  662.5 1.3 copy-start
  681.8 11.2 %copy-start.1 = (bf16[896,4,48]{0,2,1:T(8,128)(2,1)S(1)}, bf16[896,4,48]{0,2,1:T(8,128)(2,1)}, u32[]{:S(2)}) copy-start(bf16[896,4,48]{0,2,1:T(8,128)(2,1)} %copy-done) | copy-start | bytes 1032196 | tf_op jit(solution)/shard_map/while
  697.3 1.3 copy-start
  716.6 11.2 %copy-start.1 = (bf16[896,4,48]{0,2,1:T(8,128)(2,1)S(1)}, bf16[896,4,48]{0,2,1:T(8,128)(2,1)}, u32[]{:S(2)}) copy-start(bf16[896,4,48]{0,2,1:T(8,128)(2,1)} %copy-done) | copy-start | bytes 1032196 | tf_op jit(solution)/shard_map/while
  751.4 11.2 %copy-start.1 = (bf16[896,4,48]{0,2,1:T(8,128)(2,1)S(1)}, bf16[896,4,48]{0,2,1:T(8,128)(2,1)}, u32[]{:S(2)}) copy-start(bf16[896,4,48]{0,2,1:T(8,128)(2,1)} %copy-done) | copy-start | bytes 1032196 | tf_op jit(solution)/shard_map/while
  786.3 11.2 %copy-start.1 = (bf16[896,4,48]{0,2,1:T(8,128)(2,1)S(1)}, bf16[896,4,48]{0,2,1:T(8,128)(2,1)}, u32[]{:S(2)}) copy-start(bf16[896,4,48]{0,2,1:T(8,128)(2,1)} %copy-done) | copy-start | bytes 1032196 | tf_op jit(solution)/shard_map/while
  821.1 11.2 %copy-start.1 = (bf16[896,4,48]{0,2,1:T(8,128)(2,1)S(1)}, bf16[896,4,48]{0,2,1:T(8,128)(2,1)}, u32[]{:S(2)}) copy-start(bf16[896,4,48]{0,2,1:T(8,128)(2,1)} %copy-done) | copy-start | bytes 1032196 | tf_op jit(solution)/shard_map/while
  855.9 11.2 %copy-start.1 = (bf16[896,4,48]{0,2,1:T(8,128)(2,1)S(1)}, bf16[896,4,48]{0,2,1:T(8,128)(2,1)}, u32[]{:S(2)}) copy-start(bf16[896,4,48]{0,2,1:T(8,128)(2,1)} %copy-done) | copy-start | bytes 1032196 | tf_op jit(solution)/shard_map/while
  871.4 119.6 %reduce-scatter.3.cloned.1.call-start = ((), (), s32[]{:S(2)}) async-start(), calls=%async_computation.15 | async-start | bytes 6193152 | tf_op jit(solution)/shard_map/reduce_scatter | solution.py:153
  874.3 57.5 %all-to-all-start.6 = ((bf16[4,224,192]{1,2,0:T(8,128)(2,1)}), bf16[4,224,192]{1,2,0:T(8,128)(2,1)S(1)}, u32[]{:S(2)}, u32[]{:S(2)}) async-start(bf16[4,224,192]{1,2,0:T(8,128)(2,1)} %copy.92), calls=%async_computation.6 | async-start | bytes 786432 | tf_op jit(solution)/shard_map/all_to_all | solution.py:160
  931.7 61.5 %all-to-all-start.8 = ((bf16[4,224,192]{1,2,0:T(8,128)(2,1)}), bf16[4,224,192]{1,2,0:T(8,128)(2,1)S(1)}, u32[]{:S(2)}, u32[]{:S(2)}) async-start(bf16[4,224,192]{1,2,0:T(8,128)(2,1)} %copy.94), calls=%async_computation.10 | async-start | bytes 786432 | tf_op jit(solution)/shard_map/all_to_all | solution.py:162
  993.2 47.7 %all-to-all-start.7 = ((bf16[4,224,192]{1,2,0:T(8,128)(2,1)}), bf16[4,224,192]{1,2,0:T(8,128)(2,1)S(1)}, u32[]{:S(2)}, u32[]{:S(2)}) async-start(bf16[4,224,192]{1,2,0:T(8,128)(2,1)} %copy.93), calls=%async_computation.8 | async-start | bytes 786432 | tf_op jit(solution)/shard_map/all_to_all | solution.py:161
  (4 other events, 5.2 us)
Sparse Core Ops, SparseCore 0:
  27.7 33.6 all-gather.6
  63.3 34.5 all-gather.8
  100.3 30.5 all-gather.4
  133.2 30.5 all-gather.10
  871.5 57.8 reduce-scatter.4
  933.1 57.8 reduce-scatter.2
where the time goes:
time: 1060 us; the launch traced here: 1050 us
  matrix products  429 us (40%)
  other arithmetic  217 us (20%)
  waiting for transfers between devices  168 us (16%)
  blocking collectives  102 us (10%)
  local copies, waits for them, and re-layouts  84.8 us (8%)
  starting transfers between devices  21 us (2%)
  between operations  16.3 us (2%)
  loops' own time  11.9 us (1%)
    dot_general x56, matrix products, logits(): jnp.einsum('rhd,chd->hrc', left, right, preferred_element_type=jnp.float32)  338 us
    reduce_sum x28, other arithmetic, stats_step(): jnp.sum(jnp.exp(score - top[..., None]), axis=-1)  212 us
    reduce_scatter x1, waiting for transfers between devices, on_device(): lax.psum_scatter(results[2], 'seq', scatter_dimension=0, tiled=True)  54.6 us
    reduce_scatter x1, waiting for transfers between devices, on_device(): lax.psum_scatter(results[3], 'seq', scatter_dimension=0, tiled=True)  50.5 us
    dynamic_slice x42, local copies, waits for them, and re-layouts, advance(): lax.dynamic_slice_in_dim(member, index * size, size, 0)  47.6 us
    psum x1, blocking collectives, on_device(): loss = lax.psum(jnp.sum(total), ('seq', 'head')) / (HEADS * total_rows)  40 us
    all_gather x1, waiting for transfers between devices, on_device(): lax.all_gather(key_set[3], 'seq', axis=0, tiled=True)  33 us
    dot_general x7, matrix products, grads_step(): jnp.einsum('hrc,rhd->chd', grad_qk, query_s, preferred_element_type=jnp.f...  30.4 us
  transfers between devices with their start and end apart: 11, of which 6 were waited for; matrix products, arithmetic and copies ran while one was open for 3% of the time, Pallas kernels for 0%

commit v1 on v0

v1 whole, which is shorter than its diff:
```python
import functools
import math

import jax
import jax.numpy as jnp
from jax import lax
from jax.experimental import pallas as pl
from jax.experimental.pallas import tpu as pltpu
from jax.sharding import PartitionSpec as P

HEADS = 16
TD = 64
SD = 48
RB = 128
LIMIT = 100.0
LOG2E = math.log2(math.e)
LN2 = math.log(2.0)
F32 = jnp.float32
BF16 = jnp.bfloat16


def pick(count, options):
    for size in options:
        if count % size == 0:
            return size
    return count


def fold(x):
    return jnp.sum(x.reshape(x.shape[0] // 8, 8, x.shape[1]), axis=0)


def fold_max(x):
    return jnp.max(x.reshape(x.shape[0] // 8, 8, x.shape[1]), axis=0)


def kernel(q_ref, k_ref, dq_ref, dk_ref, kl_ref, kt_ref, cm_ref, e_ref, st_ref):
    count = k_ref.shape[0]
    first = pick(count, (512, 256, 128, 64, 32, 16, 8))
    second = pick(count, (1024, 512, 256, 128))
    tfac = TD ** (-0.5) * LOG2E
    sfac = SD ** (-0.5) * LOG2E
    sscale = SD ** (-0.5)

    @pl.when(pl.program_id(1) == 0)
    def _():
        dk_ref[...] = jnp.zeros_like(dk_ref)
        part = pick(count, (1024, 512, 256, 128))

        def prepare(i, tops):
            here = pl.ds(pl.multiple_of(i * part, part), part)
            x = k_ref[here, :].astype(F32)
            kt_ref[64:128, here] = x[:, :128].T[64:, :].astype(BF16)
            kt_ref[0:64, here] = x[:, 128:].T[64:, :].astype(BF16)
            return jnp.maximum(tops, fold_max(jnp.abs(x)))

        tops = lax.fori_loop(0, count // part, prepare, jnp.zeros((8, 256), F32))
        tops = jnp.max(tops, axis=0, keepdims=True)
        cm_ref[...] = jnp.broadcast_to(tops, cm_ref.shape)

    q = q_ref[...].astype(F32)
    lane = lax.broadcasted_iota(jnp.int32, (RB, 128), 1)
    row = lax.broadcasted_iota(jnp.int32, (128, RB), 0)

    def weights(block):
        t = block.T
        t = jnp.concatenate(
            [jnp.where(row < TD, t, 0.0), jnp.where(row < TD, 0.0, t)], axis=1
        )
        return t

    raw_k, raw_v = weights(q[:, :128]), weights(q[:, 128:])
    col = lax.broadcasted_iota(jnp.int32, (1, 256), 1)
    factor = jnp.where(col < RB, tfac, sfac)
    full_k, full_v = raw_k * factor, raw_v * factor
    bound_k = jnp.dot(
        cm_ref[:, :128].astype(BF16), jnp.abs(raw_k).astype(BF16), preferred_element_type=F32
    )
    bound_v = jnp.dot(
        cm_ref[:, 128:].astype(BF16), jnp.abs(raw_v).astype(BF16), preferred_element_type=F32
    )
    bound = jnp.max(jnp.maximum(bound_k * factor, bound_v * factor))

    zero = jnp.zeros((8, RB), F32)

    def total(x):
        return jnp.broadcast_to(jnp.sum(x, axis=0, keepdims=True), x.shape)

    @pl.when(bound <= LIMIT)
    def _():
        def split(w):
            high = w.astype(BF16)
            low = (w - high.astype(F32)).astype(BF16)
            return jnp.concatenate([high, low], axis=0)

        wk, wv = split(full_k), split(full_v)

        def step(i, carry):
            za, zc, s, zb, ze, u = carry
            here = pl.ds(pl.multiple_of(i * first, first), first)
            xk = k_ref[here, :128]
            xv = k_ref[here, 128:]
            lk = jnp.dot(jnp.concatenate([xk, xk], axis=1), wk, preferred_element_type=F32)
            lv = jnp.dot(jnp.concatenate([xv, xv], axis=1), wv, preferred_element_type=F32)
            a, c, b, e = lk[:, :RB], lk[:, RB:], lv[:, :RB], lv[:, RB:]
            pa, pc, pb, pe = jnp.exp2(a), jnp.exp2(c), jnp.exp2(b), jnp.exp2(e)
            e_ref[here, 0:128] = pa.astype(e_ref.dtype)
            e_ref[here, 128:256] = pc.astype(e_ref.dtype)
            e_ref[here, 256:384] = pb.astype(e_ref.dtype)
            e_ref[here, 384:512] = pe.astype(e_ref.dtype)
            return (
                za + fold(pa), zc + fold(pc), s + fold(pa * (a - c)),
                zb + fold(pb), ze + fold(pe), u + fold(pb * (b - e)),
            )

        out = lax.fori_loop(0, count // first, step, (zero,) * 6)
        for n, value in enumerate(out):
            st_ref[n] = total(value)

    @pl.when(jnp.logical_not(bound <= LIMIT))
    def _():
        wk, wv = raw_k.astype(BF16), raw_v.astype(BF16)

        def blocks(i):
            here = pl.ds(pl.multiple_of(i * first, first), first)
            lk = jnp.dot(k_ref[here, :128], wk, preferred_element_type=F32)
            lv = jnp.dot(k_ref[here, 128:], wv, preferred_element_type=F32)
            return here, (
                lk[:, :RB] * tfac, lk[:, RB:] * sfac, lv[:, :RB] * tfac, lv[:, RB:] * sfac
            )

        def peak(i, tops):
            _, parts = blocks(i)
            return tuple(jnp.maximum(t, fold_max(p)) for t, p in zip(tops, parts))

        tops = lax.fori_loop(
            0, count // first, peak, (jnp.full((8, RB), -3e38, F32),) * 4
        )
        tops = tuple(jnp.max(t, axis=0, keepdims=True) for t in tops)

        def step(i, carry):
            za, zc, s, zb, ze, u = carry
            here, parts = blocks(i)
            a, c, b, e = (p - t for p, t in zip(parts, tops))
            pa, pc, pb, pe = jnp.exp2(a), jnp.exp2(c), jnp.exp2(b), jnp.exp2(e)
            e_ref[here, 0:128] = pa.astype(e_ref.dtype)
            e_ref[here, 128:256] = pc.astype(e_ref.dtype)
            e_ref[here, 256:384] = pb.astype(e_ref.dtype)
            e_ref[here, 384:512] = pe.astype(e_ref.dtype)
            return (
                za + fold(pa), zc + fold(pc), s + fold(pa * (a - c)),
                zb + fold(pb), ze + fold(pe), u + fold(pb * (b - e)),
            )

        out = lax.fori_loop(0, count // first, step, (zero,) * 6)
        for n, value in enumerate(out):
            st_ref[n] = total(value)

    za, zc, s, zb, ze, u = (st_ref[n] for n in range(6))
    kl_ref[...] = (
        s / za - jnp.log2(za) + jnp.log2(zc) + u / zb - jnp.log2(zb) + jnp.log2(ze)
    ) * LN2
    ia, ic, ib, ie = (1.0 / z[0:1, :] for z in (za, zc, zb, ze))

    only_k = jnp.where(lane < TD, 0.0, q[:, :128])
    only_v = pltpu.roll(jnp.where(lane < TD, 0.0, q[:, 128:]), 64, 1)
    wd = jnp.concatenate([only_k, only_v], axis=0).astype(BF16)

    def grads(i, acc):
        here = pl.ds(pl.multiple_of(i * second, second), second)
        gk = (e_ref[here, 128:256] * ic - e_ref[here, 0:128] * ia).astype(BF16)
        gv = (e_ref[here, 384:512] * ie - e_ref[here, 256:384] * ib).astype(BF16)
        g = jnp.concatenate([gk, gv], axis=1)
        dk_ref[here, :] += jnp.dot(g, wd, preferred_element_type=F32)
        return acc + jnp.dot(kt_ref[:, here], g, preferred_element_type=F32)

    acc = lax.fori_loop(0, count // second, grads, jnp.zeros((128, 256), F32))
    d = jnp.where(row < TD, acc[:, RB:], acc[:, :RB])
    dq_ref[...] = d.T * sscale

    @pl.when(pl.program_id(1) == pl.num_programs(1) - 1)
    def _():
        dk_ref[...] = dk_ref[...] * sscale


def relation(q, k, local_heads):
    rows, count = q.shape[0], k.shape[0]
    turns = rows // RB
    return pl.pallas_call(
        kernel,
        out_shape=(
            jax.ShapeDtypeStruct((rows, local_heads * 128), F32),
            jax.ShapeDtypeStruct((count, local_heads * 128), F32),
            jax.ShapeDtypeStruct((8, local_heads * rows), F32),
        ),
        grid_spec=pltpu.PrefetchScalarGridSpec(
            num_scalar_prefetch=0,
            grid=(local_heads, turns),
            in_specs=[
                pl.BlockSpec((RB, 256), lambda h, r: (r, h)),
                pl.BlockSpec((count, 256), lambda h, r: (0, h)),
            ],
            out_specs=[
                pl.BlockSpec((RB, 128), lambda h, r: (r, h)),
                pl.BlockSpec((count, 128), lambda h, r: (0, h)),
                pl.BlockSpec((8, RB), lambda h, r: (0, h * turns + r)),
            ],
            scratch_shapes=[
                pltpu.VMEM((128, count), BF16),
                pltpu.VMEM((8, 256), F32),
                pltpu.VMEM((count, 512), F32),
                pltpu.VMEM((6, 8, RB), F32),
            ],
        ),
        compiler_params=pltpu.CompilerParams(
            dimension_semantics=("arbitrary", "arbitrary"), vmem_limit_bytes=58 << 20
        ),
        cost_estimate=pl.CostEstimate(
            flops=int(local_heads * rows * count * 2 * 1024),
            bytes_accessed=int(local_heads * count * 1024),
            transcendentals=int(local_heads * rows * count * 4),
        ),
    )(q, k)


def on_device(teacher_query, teacher_key, teacher_value, student_query, student_key, student_value):
    tokens = teacher_query.shape[0]

    def pack(teacher, student):
        return jnp.concatenate(
            [
                teacher.reshape(tokens, HEADS, TD),
                student.reshape(tokens, HEADS, SD),
                jnp.zeros((tokens, HEADS, 128 - TD - SD), BF16),
            ],
            axis=2,
        )

    packed = jnp.concatenate(
        [
            pack(teacher_query, student_query),
            pack(teacher_key, student_key),
            pack(teacher_value, student_value),
        ],
        axis=2,
    ).reshape(tokens, HEADS * 384)
    mine = lax.all_to_all(packed, "head", split_axis=1, concat_axis=0, tiled=True)
    rows = mine.shape[0]
    local_heads = mine.shape[1] // 384
    total_rows = rows * lax.axis_size("seq")
    mine = mine.reshape(rows, local_heads, 384)
    keys = mine[:, :, 128:].reshape(rows, local_heads * 256)
    queries = jnp.concatenate([mine[:, :, :128], mine[:, :, 256:]], axis=2)
    queries = queries.reshape(rows, local_heads * 256)
    padded = -(-rows // RB) * RB
    queries = jnp.pad(queries, ((0, padded - rows), (0, 0)))
    keys = lax.all_gather(keys, "seq", axis=0, tiled=True)
    dq, dk, kl = relation(queries, keys, local_heads)
    kl = jnp.sum(kl[0].reshape(local_heads, padded)[:, :rows])
    loss = lax.psum(kl, ("seq", "head")) / (HEADS * total_rows)

    dk = dk.reshape(total_rows, local_heads, 128)
    dk = jnp.concatenate([dk[:, :, TD : TD + SD], dk[:, :, :SD]], axis=2)
    dk = dk.reshape(total_rows, local_heads * 2 * SD)
    owned = lax.psum_scatter(dk, "seq", scatter_dimension=0, tiled=True)
    owned = owned.reshape(rows, local_heads, 2 * SD)
    dq = dq[:rows].reshape(rows, local_heads, 128)
    out = jnp.concatenate(
        [dq[:, :, TD : TD + SD], owned[:, :, :SD], owned[:, :, SD:] + dq[:, :, :SD]], axis=2
    ).astype(BF16)
    out = out.reshape(rows, local_heads * 3 * SD)
    out = lax.all_to_all(out, "head", split_axis=0, concat_axis=1, tiled=True)
    out = out.reshape(tokens, HEADS, 3, SD)
    return tuple(out[:, :, n].reshape(tokens, HEADS * SD) for n in range(3)) + (loss,)


def solution(mesh):
    spec = P(("seq", "head"), None)
    return jax.shard_map(
        on_device, mesh=mesh, in_specs=(spec,) * 6, out_specs=(spec, spec, spec, P()),
        check_vma=False,
    )
```

time: 1060 us -> 714 us (0.67)
  matrix products: 429 us -> 0 us
  Pallas kernels: 0 us -> 352 us
  other arithmetic: 217 us -> 13.4 us
  local copies, waits for them, and re-layouts: 84.8 us -> 53 us
  starting transfers between devices: 21 us -> 4.68 us
  blocking collectives: 102 us -> 114 us
  loops' own time: 11.9 us -> 0 us
    dot_general x84 -> x0, matrix products: 429 us -> none  [the longest x56 338 us: logits(): jnp.einsum('rhd,chd->hrc', left, right, preferred_element_type=jnp.float32)]
    pallas_call x0 -> x1, Pallas kernels: none -> 352 us  [relation(): pl.pallas_call(kernel, out_shape=(jax.ShapeDtypeStruct((rows, local_heads...]
    reduce_sum x29 -> x1, other arithmetic: 213 us -> 1.53 us  [on_device(): kl = jnp.sum(kl[0].reshape(local_heads, padded)[:, :rows])]
    dynamic_slice x42 -> x0, local copies, waits for them, and re-layouts: 47.6 us -> none  [advance(): lax.dynamic_slice_in_dim(member, index * size, size, 0)]
    all_gather x4 -> x1, waiting for transfers between devices: 43.5 us -> 77.1 us  [on_device(): keys = lax.all_gather(keys, 'seq', axis=0, tiled=True)]
    reduce_scatter x2 -> x1, waiting for transfers between devices: 105 us -> 82.3 us  [on_device(): owned = lax.psum_scatter(dk, 'seq', scatter_dimension=0, tiled=True)]
    reshape x4 -> x3, local copies, waits for them, and re-layouts: 1.31 us -> 20.8 us  [the longest x1 14.4 us: on_device(): dk = dk.reshape(total_rows, local_heads, 128)]
    all_to_all x5 -> x1, waiting for transfers between devices: 18.9 us -> 0.01 us  [on_device(): out = lax.all_to_all(out, 'head', split_axis=0, concat_axis=1, tiled=True)]
  transfers between devices with their start and end apart: 11 -> 3, of which waited for: 6 -> 2; matrix products, arithmetic and copies ran while one was open for 3% -> 1% of each run, Pallas kernels for 0% -> 0%
where the time goes in v1:
time: 714 us; the launch traced here: 713 us
  Pallas kernels  352 us (49%)
  waiting for transfers between devices  159 us (22%)
  blocking collectives  114 us (16%)
  local copies, waits for them, and re-layouts  53 us (7%)
  between operations  16.1 us (2%)
  other arithmetic  13.4 us (2%)
    pallas_call x1, Pallas kernels, relation(): pl.pallas_call(kernel, out_shape=(jax.ShapeDtypeStruct((rows, local_heads...  352 us
    reduce_scatter x1, waiting for transfers between devices, on_device(): owned = lax.psum_scatter(dk, 'seq', scatter_dimension=0, tiled=True)  82.3 us
    all_gather x1, waiting for transfers between devices, on_device(): keys = lax.all_gather(keys, 'seq', axis=0, tiled=True)  77.1 us
    all_to_all x1, blocking collectives, on_device(): lax.all_to_all(packed, 'head', split_axis=1, concat_axis=0, tiled=True)  68.5 us
    psum x1, blocking collectives, on_device(): loss = lax.psum(kl, ('seq', 'head')) / (HEADS * total_rows)  45.6 us
    reshape x1, local copies, waits for them, and re-layouts, on_device(): dk = dk.reshape(total_rows, local_heads, 128)  14.4 us
  transfers between devices with their start and end apart: 3, of which 2 were waited for; matrix products, arithmetic and copies ran while one was open for 1% of the time, Pallas kernels for 0%

profile of v1, /device:TPU:0, one launch (start us, length us, event | category | flops | bytes accessed | tf_op | source)
XLA Modules:
  0.0 713.1 jit_solution(12186231675137721617)
XLA Ops:
  7.2 1.2 copy.27
  8.5 1.1 copy.29
  9.6 1.1 copy.31
  10.8 1.2 copy.26
  12.8 1.6 copy-done
  14.4 3.1 copy.32
  17.6 68.5 %all_to_all.29 = bf16[224,4,1536]{2,0,1:T(8,128)(2,1)} all-to-all(bf16[224,4,1536]{2,0,1:T(8,128)(2,1)S(1)} %copy.32), channel_id=1, replica_groups=mesh['seq'=8,'head'=4] {'head'}, dimensions={1} | all-to-all | bytes 5505024 | tf_op jit(solution)/shard_map/all_to_all | solution.py:247
  86.0 4.6 reshape.70
  91.3 1.6 copy.45
  94.6 1.7 copy.44
  96.3 77.1 %all-gather.2.cloned.1.call-done.k_ref = bf16[7168,1024]{1,0:T(8,128)(2,1)} async-done(((bf16[896,1024]{1,0:T(8,128)(2,1)}), bf16[7168,1024]{1,0:T(8,128)(2,1)}) %all-gather.2.cloned.1.call-update) | async-done | bytes 14680080 | tf_op jit(solution)/shard_map/all_gather | solution.py:257
  173.4 352.4 %shard_map.93 = (f32[896,512]{1,0:T(8,128)}, f32[7168,512]{1,0:T(8,128)}, f32[8,3584]{1,0:T(8,128)}) custom-call(bf16[896,1024]{1,0:T(8,128)(2,1)} %bitcast.37, bf16[7168,1024]{1,0:T(8,128)(2,1)} %all-gather.2.cloned.1.call-done.k_ref), custom_call_target="tpu_custom_call" | custom-call | flops 52613349376 | bytes 29360128 | tf_op jit(solution)/shard_map/pallas_call | solution.py:189
  525.8 14.4 %copy.43 = f32[7168,512]{0,1:T(8,128)} copy(f32[7168,512]{1,0:T(8,128)} %get-tuple-element.8) | data formatting | bytes 29360128 | tf_op jit(solution)/shard_map/reshape | solution.py:262
  540.1 9.5 %fusion.1 = (f32[7168,4,48]{0,2,1:T(8,128)}, f32[7168,4,48]{0,2,1:T(8,128)}) fusion(f32[7168,4,128]{0,2,1:T(8,128)} %bitcast.24), kind=kLoop, calls=%fused_computation.17 | loop fusion | bytes 22020096 | tf_op jit(solution)/shard_map/slice | solution.py:263
  549.6 9.6 %pad_maximum_fusion = f32[7168,4,96]{0,2,1:T(8,128)} fusion(f32[7168,4,48]{0,2,1:T(8,128)} %get-tuple-element.19, f32[7168,4,48]{0,2,1:T(8,128)} %get-tuple-element.18), kind=kLoop, calls=%fused_computation | loop fusion | flops 2752512 | bytes 22020096 | tf_op jit(solution)/shard_map/concatenate | solution.py:263
  559.2 1.8 copy.42
  561.1 82.3 %reduce-scatter.2.cloned.1.call-done = f32[896,384]{0,1:T(8,128)} async-done(((f32[7168,384]{0,1:T(8,128)}), f32[896,384]{0,1:T(8,128)}) %reduce-scatter.2.cloned.1.call-update) | async-done | bytes 1376272 | tf_op jit(solution)/shard_map/reduce_scatter | solution.py:265
  643.4 1.2 fusion
  644.6 1.1 slice.73
  645.8 1.1 convert_element_type.6
  646.9 2.4 copy.37
  649.2 4.6 all-to-all-start.1
  653.9 1.5 slice_reduce_fusion
  655.4 45.6 %psum.7 = f32[]{:T(128)} all-reduce(f32[]{:T(128)} %slice_reduce_fusion), channel_id=1, replica_groups=mesh['seq'=8,'head'=4] {'seq','head'}, use_global_device_ids=true, to_apply=%region_2.3 | all-reduce | flops 1 | bytes 8 | tf_op jit(solution)/shard_map/psum | solution.py:260
  (31 shorter events, 6.6 us)
Async XLA Ops:
  7.2 4.8 copy-start.1
  7.2 5.0 copy-start.2
  7.2 166.2 %all-gather.2.cloned.1.call-start = ((), (), s32[]{:S(2)}) async-start(), calls=%async_computation.3 | async-start | bytes 16515072 | tf_op jit(solution)/shard_map/all_gather | solution.py:257
  12.7 1.7 copy-start
  92.9 550.5 %reduce-scatter.2.cloned.1.call-start = ((), (), s32[]{:S(2)}) async-start(), calls=%async_computation.4 | async-start | bytes 12386304 | tf_op jit(solution)/shard_map/reduce_scatter | solution.py:265
  649.2 52.4 %all-to-all-start.1 = ((bf16[4,224,576]{2,1,0:T(8,128)(2,1)}), bf16[4,224,576]{2,1,0:T(8,128)(2,1)S(1)}, u32[]{:S(2)}, u32[]{:S(2)}) async-start(bf16[4,224,576]{2,1,0:T(8,128)(2,1)} %copy.37), calls=%async_computation.2 | async-start | bytes 2293760 | tf_op jit(solution)/shard_map/all_to_all | solution.py:272
Sparse Core Ops, SparseCore 0:
  93.1 80.2 all-gather.1
  559.4 83.9 reduce-scatter.1

commit v2 on v1

--- a/solution.py
+++ b/solution.py
@@ -34,10 +34,10 @@
     return jnp.max(x.reshape(x.shape[0] // 8, 8, x.shape[1]), axis=0)
 
 
-def kernel(q_ref, k_ref, dq_ref, dk_ref, kl_ref, kt_ref, cm_ref, e_ref, st_ref):
+def kernel(rows, q_ref, k_ref, dq_ref, dk_ref, kt_ref, cm_ref, e_ref, st_ref, kl_ref):
     count = k_ref.shape[0]
-    first = pick(count, (512, 256, 128, 64, 32, 16, 8))
-    second = pick(count, (1024, 512, 256, 128))
+    first = pick(count, (1792, 1024, 512, 256, 128))
+    second = pick(count, (3584, 1024, 512, 256, 128))
     tfac = TD ** (-0.5) * LOG2E
     sfac = SD ** (-0.5) * LOG2E
     sscale = SD ** (-0.5)
@@ -157,9 +157,10 @@
             st_ref[n] = total(value)
 
     za, zc, s, zb, ze, u = (st_ref[n] for n in range(6))
-    kl_ref[...] = (
-        s / za - jnp.log2(za) + jnp.log2(zc) + u / zb - jnp.log2(zb) + jnp.log2(ze)
-    ) * LN2
+    kl = (s / za - jnp.log2(za) + jnp.log2(zc) + u / zb - jnp.log2(zb) + jnp.log2(ze)) * LN2
+    place = pl.program_id(1) * RB + lax.broadcasted_iota(jnp.int32, (8, RB), 1)
+    kl = jnp.sum(jnp.where(place < rows, kl, 0.0)) * 0.125
+    kl_ref[0, 0] = jnp.where(pl.program_id(1) == 0, 0.0, kl_ref[0, 0]) + kl
     ia, ic, ib, ie = (1.0 / z[0:1, :] for z in (za, zc, zb, ze))
 
     only_k = jnp.where(lane < TD, 0.0, q[:, :128])
@@ -180,22 +181,28 @@
 
     @pl.when(pl.program_id(1) == pl.num_programs(1) - 1)
     def _():
-        dk_ref[...] = dk_ref[...] * sscale
-
-
-def relation(q, k, local_heads):
+        last = lax.broadcasted_iota(jnp.int32, (1, 128), 1) == 127
+
+        def finish(i, _):
+            here = pl.ds(pl.multiple_of(i * second, second), second)
+            dk_ref[here, :] = jnp.where(last, kl_ref[0, 0], dk_ref[here, :] * sscale)
+            return 0
+
+        lax.fori_loop(0, count // second, finish, 0)
+
+
+def relation(q, k, valid):
     rows, count = q.shape[0], k.shape[0]
-    turns = rows // RB
+    local_heads = q.shape[1] // 256
     return pl.pallas_call(
-        kernel,
+        functools.partial(kernel, valid),
         out_shape=(
             jax.ShapeDtypeStruct((rows, local_heads * 128), F32),
             jax.ShapeDtypeStruct((count, local_heads * 128), F32),
-            jax.ShapeDtypeStruct((8, local_heads * rows), F32),
         ),
         grid_spec=pltpu.PrefetchScalarGridSpec(
             num_scalar_prefetch=0,
-            grid=(local_heads, turns),
+            grid=(local_heads, rows // RB),
             in_specs=[
                 pl.BlockSpec((RB, 256), lambda h, r: (r, h)),
                 pl.BlockSpec((count, 256), lambda h, r: (0, h)),
@@ -203,17 +210,17 @@
             out_specs=[
                 pl.BlockSpec((RB, 128), lambda h, r: (r, h)),
                 pl.BlockSpec((count, 128), lambda h, r: (0, h)),
-                pl.BlockSpec((8, RB), lambda h, r: (0, h * turns + r)),
             ],
             scratch_shapes=[
                 pltpu.VMEM((128, count), BF16),
                 pltpu.VMEM((8, 256), F32),
                 pltpu.VMEM((count, 512), F32),
                 pltpu.VMEM((6, 8, RB), F32),
+                pltpu.SMEM((1, 1), F32),
             ],
         ),
         compiler_params=pltpu.CompilerParams(
-            dimension_semantics=("arbitrary", "arbitrary"), vmem_limit_bytes=58 << 20
+            dimension_semantics=("arbitrary", "arbitrary"), vmem_limit_bytes=52 << 20
         ),
         cost_estimate=pl.CostEstimate(
             flops=int(local_heads * rows * count * 2 * 1024),
@@ -225,53 +232,50 @@
 
 def on_device(teacher_query, teacher_key, teacher_value, student_query, student_key, student_value):
     tokens = teacher_query.shape[0]
-
-    def pack(teacher, student):
-        return jnp.concatenate(
-            [
-                teacher.reshape(tokens, HEADS, TD),
-                student.reshape(tokens, HEADS, SD),
-                jnp.zeros((tokens, HEADS, 128 - TD - SD), BF16),
-            ],
-            axis=2,
-        )
-
-    packed = jnp.concatenate(
-        [
-            pack(teacher_query, student_query),
-            pack(teacher_key, student_key),
-            pack(teacher_value, student_value),
-        ],
-        axis=2,
-    ).reshape(tokens, HEADS * 384)
+    blank = jnp.zeros((tokens, 128 - TD - SD), BF16)
+    pairs = (
+        (teacher_query, student_query),
+        (teacher_key, student_key),
+        (teacher_value, student_value),
+    )
+    pieces = []
+    for h in range(HEADS):
+        for teacher, student in pairs:
+            pieces += [teacher[:, h * TD : (h + 1) * TD], student[:, h * SD : (h + 1) * SD], blank]
+    packed = jnp.concatenate(pieces, axis=1)
     mine = lax.all_to_all(packed, "head", split_axis=1, concat_axis=0, tiled=True)
     rows = mine.shape[0]
     local_heads = mine.shape[1] // 384
     total_rows = rows * lax.axis_size("seq")
-    mine = mine.reshape(rows, local_heads, 384)
-    keys = mine[:, :, 128:].reshape(rows, local_heads * 256)
-    queries = jnp.concatenate([mine[:, :, :128], mine[:, :, 256:]], axis=2)
-    queries = queries.reshape(rows, local_heads * 256)
     padded = -(-rows // RB) * RB
-    queries = jnp.pad(queries, ((0, padded - rows), (0, 0)))
-    keys = lax.all_gather(keys, "seq", axis=0, tiled=True)
-    dq, dk, kl = relation(queries, keys, local_heads)
-    kl = jnp.sum(kl[0].reshape(local_heads, padded)[:, :rows])
-    loss = lax.psum(kl, ("seq", "head")) / (HEADS * total_rows)
-
-    dk = dk.reshape(total_rows, local_heads, 128)
-    dk = jnp.concatenate([dk[:, :, TD : TD + SD], dk[:, :, :SD]], axis=2)
-    dk = dk.reshape(total_rows, local_heads * 2 * SD)
-    owned = lax.psum_scatter(dk, "seq", scatter_dimension=0, tiled=True)
-    owned = owned.reshape(rows, local_heads, 2 * SD)
-    dq = dq[:rows].reshape(rows, local_heads, 128)
-    out = jnp.concatenate(
-        [dq[:, :, TD : TD + SD], owned[:, :, :SD], owned[:, :, SD:] + dq[:, :, :SD]], axis=2
-    ).astype(BF16)
-    out = out.reshape(rows, local_heads * 3 * SD)
+    shares = []
+    for h in range(local_heads):
+        block = mine[:, h * 384 : (h + 1) * 384]
+        keys = lax.all_gather(block[:, 128:], "seq", axis=0, tiled=True)
+        queries = jnp.concatenate([block[:, :128], block[:, 256:]], axis=1)
+        queries = jnp.pad(queries, ((0, padded - rows), (0, 0)))
+        dq, dk = relation(queries, keys, rows)
+        owned = lax.psum_scatter(dk, "seq", scatter_dimension=0, tiled=True)
+        loss = owned[:, 127:]
+        high = loss.astype(BF16)
+        low = (loss - high.astype(F32)).astype(BF16)
+        dq = dq[:rows]
+        grads = jnp.concatenate(
+            [dq[:, TD : TD + SD], owned[:, TD : TD + SD], owned[:, :SD] + dq[:, :SD]], axis=1
+        )
+        shares += [grads.astype(BF16), high, low]
+    out = jnp.concatenate(shares, axis=1)
     out = lax.all_to_all(out, "head", split_axis=0, concat_axis=1, tiled=True)
-    out = out.reshape(tokens, HEADS, 3, SD)
-    return tuple(out[:, :, n].reshape(tokens, HEADS * SD) for n in range(3)) + (loss,)
+    width = 3 * SD + 2
+    outs = tuple(
+        jnp.concatenate(
+            [out[:, h * width + n * SD : h * width + (n + 1) * SD] for h in range(HEADS)], axis=1
+        )
+        for n in range(3)
+    )
+    sums = [out[0, h * width + 3 * SD : (h + 1) * width].astype(F32) for h in range(HEADS)]
+    loss = jnp.sum(jnp.stack(sums)) / (HEADS * total_rows)
+    return outs + (loss,)
 
 
 def solution(mesh):

time: 714 us -> 519 us (0.73)
  Pallas kernels: 352 us -> 263 us
  waiting for transfers between devices: 159 us -> 71.3 us
  blocking collectives: 114 us -> 101 us
  between operations: 16.1 us -> 25.5 us
  local copies, waits for them, and re-layouts: 53 us -> 44.6 us
    pallas_call x1 -> x4, Pallas kernels: 352 us -> 263 us  [relation(): pl.pallas_call(functools.partial(kernel, valid), out_shape=(jax.ShapeDtyp...]
    all_gather x1 -> x4, waiting for transfers between devices: 77.1 us -> 30.8 us  [on_device(): keys = lax.all_gather(block[:, 128:], 'seq', axis=0, tiled=True)]
    psum x1 -> x0, blocking collectives: 45.6 us -> none  [on_device(): loss = lax.psum(kl, ('seq', 'head')) / (HEADS * total_rows)]
    reduce_scatter x1 -> x4, waiting for transfers between devices: 82.3 us -> 38.5 us  [on_device(): owned = lax.psum_scatter(dk, 'seq', scatter_dimension=0, tiled=True)]
    all_to_all x0 -> x1, blocking collectives: none -> 32.2 us  [on_device(): out = lax.all_to_all(out, 'head', split_axis=0, concat_axis=1, tiled=True)]
    reshape x3 -> x0, local copies, waits for them, and re-layouts: 20.8 us -> none  [the longest x1 14.4 us: on_device(): dk = dk.reshape(total_rows, local_heads, 128)]
    concatenate x1 -> x5, local copies, waits for them, and re-layouts: 0.01 us -> 19.8 us  [the longest x1 9.31 us: on_device(): packed = jnp.concatenate(pieces, axis=1)]
    unnamed x25 -> x28, local copies, waits for them, and re-layouts: 13 us -> 1.72 us
  transfers between devices with their start and end apart: 3 -> 8, of which waited for: 2 -> 2; matrix products, arithmetic and copies ran while one was open for 1% -> 3% of each run, Pallas kernels for 0% -> 51%
where the time goes in v2:
time: 519 us; the launch traced here: 517 us
  Pallas kernels  263 us (51%)
  blocking collectives  101 us (19%)
  waiting for transfers between devices  71.3 us (14%)
  local copies, waits for them, and re-layouts  44.6 us (9%)
  between operations  25.5 us (5%)
  other arithmetic  11.8 us (2%)
    pallas_call x4, Pallas kernels, relation(): pl.pallas_call(functools.partial(kernel, valid), out_shape=(jax.ShapeDtyp...  263 us
    all_to_all x1, blocking collectives, on_device(): lax.all_to_all(packed, 'head', split_axis=1, concat_axis=0, tiled=True)  68.4 us
    reduce_scatter x4, waiting for transfers between devices, on_device(): owned = lax.psum_scatter(dk, 'seq', scatter_dimension=0, tiled=True)  38.5 us
    all_to_all x1, blocking collectives, on_device(): out = lax.all_to_all(out, 'head', split_axis=0, concat_axis=1, tiled=True)  32.2 us
    all_gather x4, waiting for transfers between devices, on_device(): keys = lax.all_gather(block[:, 128:], 'seq', axis=0, tiled=True)  30.8 us
  transfers between devices with their start and end apart: 8, of which 2 were waited for; matrix products, arithmetic and copies ran while one was open for 3% of the time, Pallas kernels for 51%

profile of v2, /device:TPU:0, one launch (start us, length us, event | category | flops | bytes accessed | tf_op | source)
XLA Modules:
  0.0 517.2 jit_solution(15343062715049714792)
XLA Ops:
  7.2 2.1 fusion.25
  9.3 2.4 fusion.26
  12.9 1.3 fusion.28
  14.2 1.2 fusion.29
  15.4 1.3 fusion.30
  16.7 9.3 %concatenate.36 = bf16[224,6144]{1,0:T(8,128)(2,1)S(1)} concatenate(bf16[224,64]{1,0:T(8,128)(2,1)} %get-tuple-element.150, bf16[224,48]{1,0:T(8,128)(2,1)} %get-tuple-element.198, bf16[224,16]{1,0:T(8,128)(2,1)S(1)} %broadcast_in_dim.3, bf16[224,64]{1,0:T(8,128)(2,1)} %get-tuple-element.134, bf16[224,48]{1,0:T(8,128)(2,1)} %get-tuple-element.182, ...), dimensions={1} | concatenate | bytes 5505024 | tf_op jit(solution)/shard_map/concatenate | solution.py:245
  26.2 68.4 %all_to_all.38 = bf16[224,4,1536]{2,0,1:T(8,128)(2,1)S(1)} all-to-all(bf16[224,4,1536]{2,0,1:T(8,128)(2,1)S(1)} %bitcast.12), channel_id=1, replica_groups=mesh['seq'=8,'head'=4] {'head'}, dimensions={1} | all-to-all | bytes 5505024 | tf_op jit(solution)/shard_map/all_to_all | solution.py:246
  94.6 1.3 fusion.20
  99.1 30.7 %all-gather.11.cloned.1.call-done.k_ref = bf16[7168,256]{1,0:T(8,128)(2,1)} async-done(((bf16[896,256]{1,0:T(8,128)(2,1)}), bf16[7168,256]{1,0:T(8,128)(2,1)}) %all-gather.11.cloned.1.call-update) | async-done | bytes 3670032 | tf_op jit(solution)/shard_map/all_gather | solution.py:254
  129.8 65.6 %shard_map.96 = (f32[896,128]{1,0:T(8,128)S(1)}, f32[7168,128]{1,0:T(8,128)}) custom-call(bf16[896,256]{1,0:T(8,128)(2,1)S(1)} %pad_maximum_fusion.3.q_ref, bf16[7168,256]{1,0:T(8,128)(2,1)} %all-gather.11.cloned.1.call-done.k_ref), custom_call_target="tpu_custom_call" | custom-call | flops 13153337344 | bytes 7340032 | tf_op jit(solution)/shard_map/pallas_call | solution.py:197
  196.6 65.7 %shard_map.95 = (f32[896,128]{1,0:T(8,128)S(1)}, f32[7168,128]{1,0:T(8,128)}) custom-call(bf16[896,256]{1,0:T(8,128)(2,1)S(1)} %pad_maximum_fusion.2.q_ref, bf16[7168,256]{1,0:T(8,128)(2,1)} %all-gather.9.cloned.1.call-done.k_ref), custom_call_target="tpu_custom_call" | custom-call | flops 13153337344 | bytes 7340032 | tf_op jit(solution)/shard_map/pallas_call | solution.py:197
  263.3 66.1 %shard_map.94 = (f32[896,128]{1,0:T(8,128)S(1)}, f32[7168,128]{1,0:T(8,128)}) custom-call(bf16[896,256]{1,0:T(8,128)(2,1)S(1)} %pad_maximum_fusion.1.q_ref, bf16[7168,256]{1,0:T(8,128)(2,1)} %all-gather.7.cloned.1.call-done.k_ref), custom_call_target="tpu_custom_call" | custom-call | flops 13153337344 | bytes 7340032 | tf_op jit(solution)/shard_map/pallas_call | solution.py:197
  329.6 65.6 %shard_map.93 = (f32[896,128]{1,0:T(8,128)S(1)}, f32[7168,128]{1,0:T(8,128)}) custom-call(bf16[896,256]{1,0:T(8,128)(2,1)S(1)} %pad_maximum_fusion.q_ref, bf16[7168,256]{1,0:T(8,128)(2,1)} %all-gather.5.cloned.1.call-done.k_ref), custom_call_target="tpu_custom_call" | custom-call | flops 13153337344 | bytes 7340032 | tf_op jit(solution)/shard_map/pallas_call | solution.py:197
  396.4 1.9 slice.964
  398.3 1.9 slice.966
  400.2 1.9 slice.968
  402.1 2.2 subtract_convert_fusion
  404.3 2.2 subtract_convert_fusion.1
  409.8 38.5 %reduce-scatter.5.cloned.1.call-done = f32[896,128]{1,0:T(8,128)} async-done(((f32[7168,128]{1,0:T(8,128)}), f32[896,128]{1,0:T(8,128)}) %reduce-scatter.5.cloned.1.call-update) | async-done | bytes 458768 | tf_op jit(solution)/shard_map/reduce_scatter | solution.py:258
  448.3 1.8 fusion.3
  450.1 1.4 subtract_convert_fusion.3
  452.7 6.3 %concatenate.41 = bf16[896,584]{1,0:T(8,128)(2,1)S(1)} concatenate(bf16[896,48]{1,0:T(8,128)(2,1)S(1)} %copy-done.10, bf16[896,48]{1,0:T(8,128)(2,1)S(1)} %slice.970, bf16[896,48]{1,0:T(8,128)(2,1)} %fusion.3, bf16[896,1]{1,0:T(8,128)(2,1)S(1)} %get-tuple-element.43, bf16[896,1]{1,0:T(8,128)(2,1)S(1)} %get-tuple-element.42, bf16[896,48]{1,0:T(8,128)(2,1)S(1)} %slice.969, ...), dimensions={1} | concatenate | bytes 2093056 | tf_op jit(solution)/shard_map/concatenate | solution.py:267
  459.0 32.2 %all_to_all.39 = bf16[4,224,584]{2,1,0:T(8,128)(2,1)S(1)} all-to-all(bf16[4,224,584]{2,1,0:T(8,128)(2,1)S(1)} %bitcast.14), channel_id=1, replica_groups=mesh['seq'=8,'head'=4] {'head'}, dimensions={0} | all-to-all | bytes 2093056 | tf_op jit(solution)/shard_map/all_to_all | solution.py:268
  505.0 1.9 concatenate.44
  (75 shorter events, 18.7 us)
Async XLA Ops:
  7.2 4.6 copy-start.6
  7.2 5.7 %copy-start.3 = (bf16[224,768]{1,0:T(8,128)(2,1)S(1)}, bf16[224,768]{1,0:T(8,128)(2,1)}, u32[]{:S(2)}) copy-start(bf16[224,768]{1,0:T(8,128)(2,1)} %param.11) | copy-start | bytes 1032196
  7.2 122.6 %all-gather.11.cloned.1.call-start = ((), (), s32[]{:S(2)}) async-start(), calls=%async_computation.12 | async-start | bytes 4128768 | tf_op jit(solution)/shard_map/all_gather | solution.py:254
  9.3 4.8 copy-start.4
  11.8 3.6 copy-start.5
  95.9 100.7 %all-gather.9.cloned.1.call-start = ((), (), s32[]{:S(2)}) async-start(), calls=%async_computation.10 | async-start | bytes 4128768 | tf_op jit(solution)/shard_map/all_gather | solution.py:254
  96.6 166.7 %all-gather.7.cloned.1.call-start = ((), (), s32[]{:S(2)}) async-start(), calls=%async_computation.8 | async-start | bytes 4128768 | tf_op jit(solution)/shard_map/all_gather | solution.py:254
  97.3 232.2 %all-gather.5.cloned.1.call-start = ((), (), s32[]{:S(2)}) async-start(), calls=%async_computation.6 | async-start | bytes 4128768 | tf_op jit(solution)/shard_map/all_gather | solution.py:254
  97.9 298.5 %reduce-scatter.11.cloned.1.call-start = ((), (), s32[]{:S(2)}) async-start(), calls=%async_computation.13 | async-start | bytes 4128768 | tf_op jit(solution)/shard_map/reduce_scatter | solution.py:258
  195.4 1.0 copy-start.8
  195.4 1.1 copy-start.9
  195.4 202.9 %reduce-scatter.9.cloned.1.call-start = ((), (), s32[]{:S(2)}) async-start(), calls=%async_computation.11 | async-start | bytes 4128768 | tf_op jit(solution)/shard_map/reduce_scatter | solution.py:258
  262.3 0.9 copy-start.7
  262.3 137.9 %reduce-scatter.7.cloned.1.call-start = ((), (), s32[]{:S(2)}) async-start(), calls=%async_computation.9 | async-start | bytes 4128768 | tf_op jit(solution)/shard_map/reduce_scatter | solution.py:258
  329.4 118.9 %reduce-scatter.5.cloned.1.call-start = ((), (), s32[]{:S(2)}) async-start(), calls=%async_computation.7 | async-start | bytes 4128768 | tf_op jit(solution)/shard_map/reduce_scatter | solution.py:258
  396.4 11.2 %copy-start = (f32[896,128]{1,0:T(8,128)S(1)}, f32[896,128]{1,0:T(8,128)}, u32[]{:S(2)}) copy-start(f32[896,128]{1,0:T(8,128)} %reduce-scatter.11.cloned.1.call-done) | copy-start | bytes 1376260
  398.3 10.0 %copy-start.1 = (f32[896,128]{1,0:T(8,128)S(1)}, f32[896,128]{1,0:T(8,128)}, u32[]{:S(2)}) copy-start(f32[896,128]{1,0:T(8,128)} %reduce-scatter.9.cloned.1.call-done) | copy-start | bytes 1376260
  400.2 6.3 %copy-start.2 = (f32[896,128]{1,0:T(8,128)S(1)}, f32[896,128]{1,0:T(8,128)}, u32[]{:S(2)}) copy-start(f32[896,128]{1,0:T(8,128)} %reduce-scatter.7.cloned.1.call-done) | copy-start | bytes 1376260
  408.3 44.3 %copy-start.10 = (bf16[896,48]{1,0:T(8,128)(2,1)S(1)}, bf16[896,48]{1,0:T(8,128)(2,1)}, u32[]{:S(2)}) copy-start(bf16[896,48]{1,0:T(8,128)(2,1)} %slice.971) | copy-start | bytes 258052
  408.3 44.3 %copy-start.11 = (bf16[896,48]{1,0:T(8,128)(2,1)S(1)}, bf16[896,48]{1,0:T(8,128)(2,1)}, u32[]{:S(2)}) copy-start(bf16[896,48]{1,0:T(8,128)(2,1)} %slice.964) | copy-start | bytes 258052
  409.1 43.6 %copy-start.12 = (bf16[896,48]{1,0:T(8,128)(2,1)S(1)}, bf16[896,48]{1,0:T(8,128)(2,1)}, u32[]{:S(2)}) copy-start(bf16[896,48]{1,0:T(8,128)(2,1)} %slice.966) | copy-start | bytes 258052
  409.1 43.6 %copy-start.13 = (bf16[896,48]{1,0:T(8,128)(2,1)S(1)}, bf16[896,48]{1,0:T(8,128)(2,1)}, u32[]{:S(2)}) copy-start(bf16[896,48]{1,0:T(8,128)(2,1)} %slice.968) | copy-start | bytes 258052
Sparse Core Ops, SparseCore 0:
  96.0 33.7 all-gather.10
  131.7 34.5 all-gather.8
  168.1 34.5 all-gather.6
  204.4 34.5 all-gather.4
  242.3 48.7 reduce-scatter.10
  294.8 48.7 reduce-scatter.8
  347.0 48.7 reduce-scatter.6
  399.6 48.6 reduce-scatter.4

commit v3 on v2

--- a/solution.py
+++ b/solution.py
@@ -34,7 +34,7 @@
     return jnp.max(x.reshape(x.shape[0] // 8, 8, x.shape[1]), axis=0)
 
 
-def kernel(rows, q_ref, k_ref, dq_ref, dk_ref, kt_ref, cm_ref, e_ref, st_ref, kl_ref):
+def kernel(rows, q_ref, k_ref, dq_ref, out_ref, kt_ref, cm_ref, e_ref, st_ref, kl_ref, dk_ref):
     count = k_ref.shape[0]
     first = pick(count, (1792, 1024, 512, 256, 128))
     second = pick(count, (3584, 1024, 512, 256, 128))
@@ -181,11 +181,16 @@
 
     @pl.when(pl.program_id(1) == pl.num_programs(1) - 1)
     def _():
-        last = lax.broadcasted_iota(jnp.int32, (1, 128), 1) == 127
+        spot = lax.broadcasted_iota(jnp.int32, (1, 128), 1)
+        rank = lax.axis_index("seq")
+        loss = jnp.full((1, 128), kl_ref[0, 0], F32)
+        high = loss.astype(BF16).astype(F32)
+        extra = jnp.where(spot < TD, high, loss - high)
+        mark = jnp.logical_or(spot == SD + rank, spot == TD + SD + rank)
 
         def finish(i, _):
             here = pl.ds(pl.multiple_of(i * second, second), second)
-            dk_ref[here, :] = jnp.where(last, kl_ref[0, 0], dk_ref[here, :] * sscale)
+            out_ref[here, :] = jnp.where(mark, extra, dk_ref[here, :] * sscale).astype(BF16)
             return 0
 
         lax.fori_loop(0, count // second, finish, 0)
@@ -198,7 +203,7 @@
         functools.partial(kernel, valid),
         out_shape=(
             jax.ShapeDtypeStruct((rows, local_heads * 128), F32),
-            jax.ShapeDtypeStruct((count, local_heads * 128), F32),
+            jax.ShapeDtypeStruct((count, local_heads * 128), BF16),
         ),
         grid_spec=pltpu.PrefetchScalarGridSpec(
             num_scalar_prefetch=0,
@@ -217,6 +222,7 @@
                 pltpu.VMEM((count, 512), F32),
                 pltpu.VMEM((6, 8, RB), F32),
                 pltpu.SMEM((1, 1), F32),
+                pltpu.VMEM((count, 128), F32),
             ],
         ),
         compiler_params=pltpu.CompilerParams(
@@ -256,7 +262,9 @@
         queries = jnp.pad(queries, ((0, padded - rows), (0, 0)))
         dq, dk = relation(queries, keys, rows)
         owned = lax.psum_scatter(dk, "seq", scatter_dimension=0, tiled=True)
-        loss = owned[:, 127:]
+        owned = owned.astype(F32)
+        loss = jnp.sum(owned[:, SD:TD], axis=1, keepdims=True)
+        loss = loss + jnp.sum(owned[:, TD + SD :], axis=1, keepdims=True)
         high = loss.astype(BF16)
         low = (loss - high.astype(F32)).astype(BF16)
         dq = dq[:rows]

time: 519 us -> 506 us (0.975)
  waiting for transfers between devices: 71.3 us -> 64.5 us
    convert_element_type x4, other arithmetic: 6.81 us -> 0.03 us  [on_device(): low = (loss - high.astype(F32)).astype(BF16)]
    reduce_scatter x4, waiting for transfers between devices: 38.5 us -> 31.8 us  [on_device(): owned = lax.psum_scatter(dk, 'seq', scatter_dimension=0, tiled=True)]
  transfers between devices with their start and end apart: 8 -> 8, of which waited for: 2 -> 2; matrix products, arithmetic and copies ran while one was open for 3% -> 2% of each run, Pallas kernels for 51% -> 52%
where the time goes in v3:
time: 506 us; the launch traced here: 505 us
  Pallas kernels  261 us (52%)
  blocking collectives  101 us (20%)
  waiting for transfers between devices  64.5 us (13%)
  local copies, waits for them, and re-layouts  42.8 us (8%)
  between operations  25.5 us (5%)
  other arithmetic  10.1 us (2%)
    pallas_call x4, Pallas kernels, relation(): pl.pallas_call(functools.partial(kernel, valid), out_shape=(jax.ShapeDtyp...  261 us
    all_to_all x1, blocking collectives, on_device(): lax.all_to_all(packed, 'head', split_axis=1, concat_axis=0, tiled=True)  68.4 us
    all_to_all x1, blocking collectives, on_device(): out = lax.all_to_all(out, 'head', split_axis=0, concat_axis=1, tiled=True)  32.2 us
    reduce_scatter x4, waiting for transfers between devices, on_device(): owned = lax.psum_scatter(dk, 'seq', scatter_dimension=0, tiled=True)  31.8 us
    all_gather x4, waiting for transfers between devices, on_device(): keys = lax.all_gather(block[:, 128:], 'seq', axis=0, tiled=True)  30.8 us
  transfers between devices with their start and end apart: 8, of which 2 were waited for; matrix products, arithmetic and copies ran while one was open for 2% of the time, Pallas kernels for 52%

profile of v3, /device:TPU:0, one launch (start us, length us, event | category | flops | bytes accessed | tf_op | source)
XLA Modules:
  0.0 504.7 jit_solution(6063524544829248812)
XLA Ops:
  7.2 2.1 fusion.25
  9.4 1.2 fusion.26
  10.6 1.1 fusion.27
  11.7 1.3 fusion.28
  12.9 1.2 fusion.29
  14.2 1.3 fusion.30
  15.4 9.3 %concatenate.65 = bf16[224,6144]{1,0:T(8,128)(2,1)S(1)} concatenate(bf16[224,64]{1,0:T(8,128)(2,1)} %get-tuple-element.158, bf16[224,48]{1,0:T(8,128)(2,1)} %get-tuple-element.206, bf16[224,16]{1,0:T(8,128)(2,1)S(1)} %broadcast_in_dim.2, bf16[224,64]{1,0:T(8,128)(2,1)} %get-tuple-element.142, bf16[224,48]{1,0:T(8,128)(2,1)} %get-tuple-element.190, ...), dimensions={1} | concatenate | bytes 5505024 | tf_op jit(solution)/shard_map/concatenate | solution.py:251
  25.0 68.4 %all_to_all.35 = bf16[224,4,1536]{2,0,1:T(8,128)(2,1)S(1)} all-to-all(bf16[224,4,1536]{2,0,1:T(8,128)(2,1)S(1)} %bitcast.23), channel_id=1, replica_groups=mesh['seq'=8,'head'=4] {'head'}, dimensions={1} | all-to-all | bytes 5505024 | tf_op jit(solution)/shard_map/all_to_all | solution.py:252
  93.4 1.3 fusion.20
  96.8 1.1 fusion.21
  97.9 30.7 %all-gather.11.cloned.1.call-done.k_ref = bf16[7168,256]{1,0:T(8,128)(2,1)} async-done(((bf16[896,256]{1,0:T(8,128)(2,1)}), bf16[7168,256]{1,0:T(8,128)(2,1)}) %all-gather.11.cloned.1.call-update) | async-done | bytes 3670032 | tf_op jit(solution)/shard_map/all_gather | solution.py:260
  128.6 65.0 %shard_map.96 = (f32[896,128]{1,0:T(8,128)S(1)}, bf16[7168,128]{1,0:T(8,128)(2,1)}) custom-call(bf16[896,256]{1,0:T(8,128)(2,1)S(1)} %pad_maximum_fusion.3.q_ref, bf16[7168,256]{1,0:T(8,128)(2,1)} %all-gather.11.cloned.1.call-done.k_ref), custom_call_target="tpu_custom_call" | custom-call | flops 13153337344 | bytes 7340032 | tf_op jit(solution)/shard_map/pallas_call | solution.py:202
  194.8 65.1 %shard_map.95 = (f32[896,128]{1,0:T(8,128)S(1)}, bf16[7168,128]{1,0:T(8,128)(2,1)}) custom-call(bf16[896,256]{1,0:T(8,128)(2,1)S(1)} %pad_maximum_fusion.2.q_ref, bf16[7168,256]{1,0:T(8,128)(2,1)} %all-gather.9.cloned.1.call-done.k_ref), custom_call_target="tpu_custom_call" | custom-call | flops 13153337344 | bytes 7340032 | tf_op jit(solution)/shard_map/pallas_call | solution.py:202
  260.9 65.4 %shard_map.94 = (f32[896,128]{1,0:T(8,128)S(1)}, bf16[7168,128]{1,0:T(8,128)(2,1)}) custom-call(bf16[896,256]{1,0:T(8,128)(2,1)S(1)} %pad_maximum_fusion.1.q_ref, bf16[7168,256]{1,0:T(8,128)(2,1)} %all-gather.7.cloned.1.call-done.k_ref), custom_call_target="tpu_custom_call" | custom-call | flops 13153337344 | bytes 7340032 | tf_op jit(solution)/shard_map/pallas_call | solution.py:202
  326.5 65.1 %shard_map.93 = (f32[896,128]{1,0:T(8,128)S(1)}, bf16[7168,128]{1,0:T(8,128)(2,1)}) custom-call(bf16[896,256]{1,0:T(8,128)(2,1)S(1)} %pad_maximum_fusion.q_ref, bf16[7168,256]{1,0:T(8,128)(2,1)} %all-gather.5.cloned.1.call-done.k_ref), custom_call_target="tpu_custom_call" | custom-call | flops 13153337344 | bytes 7340032 | tf_op jit(solution)/shard_map/pallas_call | solution.py:202
  393.8 1.0 convert_element_type.256
  394.8 1.0 convert_element_type.252
  399.7 31.8 %reduce-scatter.5.cloned.1.call-done = bf16[896,128]{1,0:T(8,128)(2,1)} async-done(((bf16[7168,128]{1,0:T(8,128)(2,1)}), bf16[896,128]{1,0:T(8,128)(2,1)}) %reduce-scatter.5.cloned.1.call-update) | async-done | bytes 229392 | tf_op jit(solution)/shard_map/reduce_scatter | solution.py:264
  440.4 5.9 %concatenate.82 = bf16[4,224,584]{2,1,0:T(8,128)(2,1)S(1)} concatenate(bf16[4,224,48]{2,1,0:T(8,128)(2,1)S(1)} %bitcast.28, bf16[4,224,48]{2,1,0:T(8,128)(2,1)} %bitcast.32, bf16[4,224,48]{2,1,0:T(8,128)(2,1)} %bitcast.36, bf16[4,224,1]{2,1,0:T(8,128)(2,1)} %copy.13, bf16[4,224,1]{2,1,0:T(8,128)(2,1)} %copy.14, bf16[4,224,48]{2,1,0:T(8,128)(2,1)S(1)} %bitcast.27, ...), dimensions={2} | concatenate | bytes 2093056 | tf_op jit(solution)/shard_map/concatenate | solution.py:275
  446.4 32.2 %all_to_all.36 = bf16[4,224,584]{2,1,0:T(8,128)(2,1)S(1)} all-to-all(bf16[4,224,584]{2,1,0:T(8,128)(2,1)S(1)} %concatenate.82), channel_id=1, replica_groups=mesh['seq'=8,'head'=4] {'head'}, dimensions={0} | all-to-all | bytes 2093056 | tf_op jit(solution)/shard_map/all_to_all | solution.py:276
  480.8 1.0 fusion.22
  492.4 1.9 concatenate.85
  494.4 1.2 concatenate.84
  495.5 1.2 concatenate.83
  (97 shorter events, 22.5 us)
Async XLA Ops:
  7.2 2.2 copy-start.3
  7.2 3.4 copy-start.4
  7.2 121.5 %all-gather.11.cloned.1.call-start = ((), (), s32[]{:S(2)}) async-start(), calls=%async_computation.12 | async-start | bytes 4128768 | tf_op jit(solution)/shard_map/all_gather | solution.py:260
  9.3 2.3 copy-start
  10.5 2.4 copy-start.1
  11.7 2.5 copy-start.2
  94.7 100.1 %all-gather.9.cloned.1.call-start = ((), (), s32[]{:S(2)}) async-start(), calls=%async_computation.10 | async-start | bytes 4128768 | tf_op jit(solution)/shard_map/all_gather | solution.py:260
  95.4 165.5 %all-gather.7.cloned.1.call-start = ((), (), s32[]{:S(2)}) async-start(), calls=%async_computation.8 | async-start | bytes 4128768 | tf_op jit(solution)/shard_map/all_gather | solution.py:260
  96.2 230.3 %all-gather.5.cloned.1.call-start = ((), (), s32[]{:S(2)}) async-start(), calls=%async_computation.6 | async-start | bytes 4128768 | tf_op jit(solution)/shard_map/all_gather | solution.py:260
  96.8 296.0 %reduce-scatter.11.cloned.1.call-start = ((), (), s32[]{:S(2)}) async-start(), calls=%async_computation.13 | async-start | bytes 2064384 | tf_op jit(solution)/shard_map/reduce_scatter | solution.py:264
  193.7 0.9 copy-start.6
  193.7 1.0 copy-start.7
  193.7 200.1 %reduce-scatter.9.cloned.1.call-start = ((), (), s32[]{:S(2)}) async-start(), calls=%async_computation.11 | async-start | bytes 2064384 | tf_op jit(solution)/shard_map/reduce_scatter | solution.py:264
  259.9 0.9 copy-start.5
  259.9 134.9 %reduce-scatter.7.cloned.1.call-start = ((), (), s32[]{:S(2)}) async-start(), calls=%async_computation.9 | async-start | bytes 2064384 | tf_op jit(solution)/shard_map/reduce_scatter | solution.py:264
  326.3 105.1 %reduce-scatter.5.cloned.1.call-start = ((), (), s32[]{:S(2)}) async-start(), calls=%async_computation.7 | async-start | bytes 2064384 | tf_op jit(solution)/shard_map/reduce_scatter | solution.py:264
  432.4 4.7 copy-start.8
  433.0 5.0 copy-start.9
  433.0 5.8 %copy-start.10 = (bf16[896,128]{1,0:T(8,128)(2,1)S(1)}, bf16[896,128]{1,0:T(8,128)(2,1)}, u32[]{:S(2)}) copy-start(bf16[896,128]{1,0:T(8,128)(2,1)} %reduce-scatter.7.cloned.1.call-done) | copy-start | bytes 688132
  433.8 5.9 %copy-start.11 = (bf16[896,128]{1,0:T(8,128)(2,1)S(1)}, bf16[896,128]{1,0:T(8,128)(2,1)}, u32[]{:S(2)}) copy-start(bf16[896,128]{1,0:T(8,128)(2,1)} %reduce-scatter.5.cloned.1.call-done) | copy-start | bytes 688132
  434.1 6.4 %copy-start.12 = (bf16[896,48]{1,0:T(8,128)(2,1)S(1)}, bf16[896,48]{1,0:T(8,128)(2,1)}, u32[]{:S(2)}) copy-start(bf16[896,48]{1,0:T(8,128)(2,1)} %slice.983) | copy-start | bytes 258052
Sparse Core Ops, SparseCore 0:
  94.8 33.7 all-gather.10
  130.5 34.5 all-gather.8
  167.0 34.5 all-gather.6
  203.3 34.5 all-gather.4
  241.0 39.7 reduce-scatter.10
  284.0 39.7 reduce-scatter.8
  327.2 39.7 reduce-scatter.6
  391.7 39.7 reduce-scatter.4
